TPU v7x, 256 devices: a whole 4x4x8 slice. The times are simulated.
256 devices in a mesh: gx: 32 (over y, z), gy: 8 (over x, core).
Axes of the slice: x: 4, y: 4, z: 8, core: 2. Of those that a mesh axis runs over, the one named last changes fastest.
Arguments:
- densities: bfloat16 [24576, 32, 128], P(('gx', 'gy')), may hold values from -6 to 6
- geometry: float32 [24576, 7, 128], P(('gx', 'gy')), as said below
- near_ids: int32 [24576, 8], P(('gx', 'gy')), may hold values from 0 to 24575, as said below
- basis_in: bfloat16 [24576, 64, 128], P(('gx', 'gy')), may hold values from -0.5 to 0.5
- basis_out: bfloat16 [24576, 64, 128], P(('gx', 'gy')), may hold values from -0.75 to 0.75
- leaf_up: bfloat16 [24576, 64, 64], P(('gx', 'gy')), may hold values from -0.078125 to 0.078125
- leaf_down: bfloat16 [24576, 64, 64], P(('gx', 'gy')), may hold values from -0.75 to 0.75
- leaf_coupling: bfloat16 [24576, 6, 64, 64], P(('gx', 'gy')), may hold values from -0.3125 to 0.3125
- leaf_far: int32 [24576, 6], P(('gx', 'gy')), may hold values from 0 to 24575, as said below
- leaf_count: int32 [24576], P(('gx', 'gy')), may hold values from 1 to 6, as said below
- cluster_up: bfloat16 [256, 64, 64], P(('gx', 'gy')), may hold values from -0.25 to 0.25
- cluster_down: bfloat16 [256, 64, 64], P(('gx', 'gy')), may hold values from -0.75 to 0.75
- cluster_coupling: bfloat16 [256, 6, 64, 64], P(('gx', 'gy')), may hold values from -0.3125 to 0.3125
- cluster_far: int32 [256, 6], P(('gx', 'gy')), may hold values from 0 to 255, as said below
- group_up: bfloat16 [32, 64, 64], replicated, may hold values from -0.375 to 0.375
- group_down: bfloat16 [32, 64, 64], P('gx'), may hold values from -0.75 to 0.75
- group_coupling: bfloat16 [32, 6, 64, 64], P('gx'), may hold values from -0.3125 to 0.3125
- group_far: int32 [32, 6], P('gx'), may hold values from 0 to 31, as said below
- root_coupling: bfloat16 [8, 8, 64, 64], replicated, may hold values from -0.25 to 0.25
Outputs:
- potential: float32 [24576, 32, 128], P(('gx', 'gy'))
Inputs may be any that keep to these rules, and one draw needn't show every extreme that they name: `near_ids`: row l names 8 different leaves of a window of 9 consecutive leaves that contains l, centred on l where the ends allow. `leaf_far`: row l names 6 different leaves held by l's device or its two neighbours in leaf order, none within 4 leaves of l; only the first leaf_count[l] entries are used. `leaf_count`: every device holds a leaf with 6. `cluster_far`: row u names 6 different level-two clusters other than u, of u's group or the two groups beside it. `group_far`: row g names 6 different level-one clusters other than g. `geometry`: rows 0 to 2 hold a panel's centre, rows 3 to 5 its unit normal, row 6 its area, from 0.25 to 2.
All inputs are finite; a program needn't handle non-finite values.
Results may differ from a plain program's by a relative error of at most 0.012.
Values may be sent and summed in bfloat16 or wider, within the bound.
A program may use at most 128 MiB of HBM per device.

v0:
```python
import math
import jax
import jax.numpy as jnp
from jax import lax
from jax.sharding import PartitionSpec as P

REACH = 4
BRANCH = 4
four_pi = 4.0 * math.pi
leaf_block = 8


def padded(cells, sides, width):
    for axis, dim in sides:
        count = lax.axis_size(axis)
        ends = count - 1
        head = lax.slice_in_dim(cells, 0, width, axis=dim)
        tail = lax.slice_in_dim(cells, cells.shape[dim] - width, cells.shape[dim], axis=dim)
        cells = jnp.concatenate(
            [
                lax.ppermute(tail, axis, [(i, (i + 1) % count) for i in range(ends)]),
                cells,
                lax.ppermute(head, axis, [((i + 1) % count, i) for i in range(ends)]),
            ],
            axis=dim,
        )
    return cells


def near_kernel(target, source):
    offsets = [
        target[:, coord_id, :, None, None] - source[:, None, :, coord_id, :]
        for coord_id in range(3)
    ]
    distance = offsets[0] * offsets[0] + offsets[1] * offsets[1] + offsets[2] * offsets[2]
    facing = (
        source[:, None, :, 3, :] * offsets[0]
        + source[:, None, :, 4, :] * offsets[1]
        + source[:, None, :, 5, :] * offsets[2]
    )
    panel_area = source[:, None, :, 6, :]
    spread = distance + panel_area
    return panel_area * facing / (four_pi * spread * jnp.sqrt(spread))


def on_device(
    densities,
    geometry,
    near_ids,
    basis_in,
    basis_out,
    leaf_up,
    leaf_down,
    leaf_coupling,
    leaf_far,
    leaf_count,
    cluster_up,
    cluster_down,
    cluster_coupling,
    cluster_far,
    group_up,
    group_down,
    group_coupling,
    group_far,
    root_coupling,
):
    wide = jnp.float32
    narrow = jnp.bfloat16
    leaves = densities.shape[0]
    coeff_order = basis_in.shape[1]
    columns = densities.shape[1]
    flat = coeff_order * columns
    first_leaf = lax.axis_index(("gx", "gy")) * leaves
    gx_index = lax.axis_index("gx")
    group_size = lax.axis_size("gy")
    groups = lax.axis_size("gx")
    leaf_coeffs = jnp.einsum(
        "lkm,lrm->lkr", basis_in, densities, preferred_element_type=wide
    ).astype(narrow)
    mid_coeffs = jnp.einsum(
        "lik,lkr->ir", leaf_up, leaf_coeffs, preferred_element_type=wide
    ).astype(narrow)
    mid_term = jnp.dot(cluster_up[0], mid_coeffs, preferred_element_type=wide).reshape(1, flat)
    mid_flat = mid_coeffs.reshape(1, flat)
    siblings = lax.all_gather(mid_flat, "gy", axis=0, tiled=True)
    group_sum = lax.psum(mid_term, "gy")
    nearby = padded(siblings, (("gx", 0),), group_size)
    mid_picked = jnp.take(nearby, cluster_far[0] - (gx_index - 1) * group_size, axis=0)
    top_coeffs = lax.all_gather(group_sum.astype(narrow), "gx", axis=0, tiled=True)
    top_block = top_coeffs.reshape(groups, coeff_order, columns)
    root_terms = jnp.einsum("gik,gkr->gir", group_up, top_block, preferred_element_type=wide)
    root_coeffs = jnp.sum(
        root_terms.reshape(groups // BRANCH, BRANCH, coeff_order, columns), axis=1
    ).astype(narrow)
    root_row = lax.dynamic_index_in_dim(root_coupling, gx_index // BRANCH, 0, keepdims=False)
    root_field = jnp.einsum(
        "sik,skr->ir", root_row, root_coeffs, preferred_element_type=wide
    ).astype(narrow)
    top_picked = jnp.take(top_block, group_far[0], axis=0)
    top_field = (
        jnp.einsum("fik,fkr->ir", group_coupling[0], top_picked, preferred_element_type=wide)
        + jnp.dot(group_down[0], root_field, preferred_element_type=wide)
    ).astype(narrow)
    mid_block = mid_picked.reshape(-1, coeff_order, columns)
    mid_field = (
        jnp.einsum("fik,fkr->ir", cluster_coupling[0], mid_block, preferred_element_type=wide)
        + jnp.dot(cluster_down[0], top_field, preferred_element_type=wide)
    ).astype(narrow)
    coeff_rim = padded(leaf_coeffs.reshape(leaves, flat), ((("gx", "gy"), 0),), leaves)
    picked = jnp.take(coeff_rim, leaf_far - (first_leaf - leaves), axis=0).reshape(
        leaves, -1, coeff_order, columns
    )
    live_mask = (lax.broadcasted_iota(jnp.int32, leaf_far.shape, 1) < leaf_count[:, None]).astype(
        narrow
    )
    picked = picked * live_mask[:, :, None, None]
    leaf_field = (
        jnp.einsum("lfik,lfkr->lir", leaf_coupling, picked, preferred_element_type=wide)
        + jnp.einsum("lik,kr->lir", leaf_down, mid_field, preferred_element_type=wide)
    ).astype(narrow)
    far_part = jnp.einsum("lkr,lkm->lrm", leaf_field, basis_out, preferred_element_type=wide)
    values_rim = padded(densities, ((("gx", "gy"), 0),), REACH)
    shape_rim = padded(geometry, ((("gx", "gy"), 0),), REACH)
    near_local = near_ids - (first_leaf - REACH)

    def near_block(pieces):
        target, indices = pieces
        source = jnp.take(shape_rim, indices, axis=0)
        values = jnp.take(values_rim, indices, axis=0)
        kernel = near_kernel(target, source).astype(narrow)
        return jnp.einsum("bmnj,bnrj->brm", kernel, values, preferred_element_type=wide)

    near_part = lax.map(
        near_block,
        (
            geometry.reshape(leaves // leaf_block, leaf_block, 7, -1),
            near_local.reshape(leaves // leaf_block, leaf_block, -1),
        ),
    )
    return far_part + near_part.reshape(far_part.shape)


def solution(mesh):
    return jax.shard_map(
        on_device,
        mesh=mesh,
        in_specs=(
            P(("gx", "gy"), None, None),
            P(("gx", "gy"), None, None),
            P(("gx", "gy"), None),
            P(("gx", "gy"), None, None),
            P(("gx", "gy"), None, None),
            P(("gx", "gy"), None, None),
            P(("gx", "gy"), None, None),
            P(("gx", "gy"), None, None, None),
            P(("gx", "gy"), None),
            P(("gx", "gy")),
            P(("gx", "gy"), None, None),
            P(("gx", "gy"), None, None),
            P(("gx", "gy"), None, None, None),
            P(("gx", "gy"), None),
            P(),
            P("gx", None, None),
            P("gx", None, None, None),
            P("gx", None),
            P(),
        ),
        out_specs=P(("gx", "gy"), None, None),
        check_vma=False,
    )
```

profile of v0, /device:TPU:8, one launch (start us, length us, event | category | flops | bytes accessed | tf_op | source)
XLA Modules:
  0.0 328.0 jit_solution(2928487035204301218)
XLA Ops:
  0.0 2.6 convolution_convert_fusion
  2.6 1.3 copy.65
  4.0 1.0 copy.66
  4.9 9.3 %collective-permute-start.1 = (bf16[96,2048]{1,0:T(8,128)(2,1)}, bf16[96,2048]{1,0:T(8,128)(2,1)}, u32[]{:S(2)}, u32[]{:S(2)}) collective-permute-start(bf16[96,2048]{1,0:T(8,128)(2,1)} %copy.66), channel_id=1, source_target_pairs={{1,0},{2,1},{3,2},{4,3},{5,4},{6,5},{7,6},{8,7},{9,8},{10,9},{11,1... | collective-permute-start | bytes 1179656 | tf_op jit(solution)/shard_map/ppermute | solution.py:23
  14.2 1.9 collective-permute-start
  16.2 1.2 copy.80
  17.4 1.9 collective-permute-start.6
  19.3 8.0 %collective-permute-start.7 = (f32[4,7,128]{2,1,0:T(8,128)S(1)}, f32[4,7,128]{2,1,0:T(8,128)S(1)}, u32[]{:S(2)}, u32[]{:S(2)}) collective-permute-start(f32[4,7,128]{2,1,0:T(8,128)S(1)} %get-tuple-element.83), channel_id=1, source_target_pairs={{1,0},{2,1},{3,2},{4,3},{5,4},{6,5},{7,6},{8,7},{9,8},{10,9},{11,1... | collective-permute-start | bytes 43016 | tf_op jit(solution)/shard_map/ppermute | solution.py:23
  27.3 4.0 %copy.72 = bf16[96,64,64]{2,1,0:T(8,128)(2,1)} copy(bf16[96,64,64]{0,2,1:T(8,128)(2,1)} %param.26) | data formatting | bytes 1572864 | tf_op args[5]
  31.4 2.0 fusion.35
  33.5 12.8 %all-gather = bf16[8,1,2048]{2,1,0:T(2,128)(2,1)S(1)} all-gather(bf16[1,1,2048]{2,1,0:T(2,128)(2,1)S(1)} %reshape.240), channel_id=1, replica_groups=mesh['gx'=32,'gy'=8] {'gy'}, dimensions={0}, use_global_device_ids=true | all-gather | bytes 36864 | tf_op jit(solution)/shard_map/all_gather | solution.py:85
  46.3 1.9 collective-permute-start.3
  48.4 0.8 fusion.62
  50.4 24.5 %psum.7 = bf16[1,2048]{1,0:T(2,128)(2,1)S(1)} all-reduce(f32[1,2048]{1,0:T(1,128)S(1)} %reshape.189), channel_id=1, replica_groups=mesh['gx'=32,'gy'=8] {'gy'}, use_global_device_ids=true, to_apply=%region_0.0 | all-reduce | flops 2048 | bytes 12288 | tf_op jit(solution)/shard_map/psum | solution.py:86
  74.9 48.0 %all-gather.1 = bf16[32,1,2048]{2,1,0:T(2,128)(2,1)S(1)} all-gather(bf16[1,1,2048]{2,1,0:T(2,128)(2,1)S(1)} %bitcast.169), channel_id=1, replica_groups=mesh['gx'=32,'gy'=8] {'gx'}, dimensions={0}, use_global_device_ids=true | all-gather | bytes 135168 | tf_op jit(solution)/shard_map/all_gather | solution.py:89
  125.1 1.1 convolution_bitcast_fusion.1
  126.2 1.8 fusion.33
  129.4 4.0 %copy.78 = bf16[96,64,64]{2,1,0:T(8,128)(2,1)} copy(bf16[96,64,64]{0,2,1:T(8,128)(2,1)} %param.27) | data formatting | bytes 1572864 | tf_op args[6]
  133.4 16.1 %copy.71 = bf16[96,6,64,64]{3,2,1,0:T(8,128)(2,1)} copy(bf16[96,6,64,64]{0,3,2,1:T(8,128)(2,1)} %param.28) | data formatting | bytes 9437184 | tf_op args[7]
  149.5 2.4 collective-permute-start.2
  152.0 1.9 collective-permute-start.4
  154.0 8.0 %collective-permute-start.5 = (bf16[4,32,128]{2,1,0:T(8,128)(2,1)S(1)}, bf16[4,32,128]{2,1,0:T(8,128)(2,1)S(1)}, u32[]{:S(2)}, u32[]{:S(2)}) collective-permute-start(bf16[4,32,128]{2,1,0:T(8,128)(2,1)S(1)} %get-tuple-element.81), channel_id=1, source_target_pairs={{1,0},{2,1},{3,2},{4,3},{5,4},{6,5},{7,6},{8,7},{9,8},{10,9},{11,1... | collective-permute-start | bytes 98312 | tf_op jit(solution)/shard_map/ppermute | solution.py:23
  163.5 1.2 pad_maximum_fusion.1
  164.7 130.7 %while.10 = (s32[]{:T(128)}, f32[12,8,32,128]{3,2,1,0:T(8,128)}, s32[12,8,8]{2,1,0:T(8,128)}, bf16[104,32,128]{2,1,0:T(8,128)(2,1)S(1)}, f32[104,7,128]{2,1,0:T(...) while((s32[]{:T(128)}, f32[12,8,32,128]{3,2,1,0:T(8,128)}, s32[12,8,8]{2,1,0:T(8,128)}, ...), condition=%wide.region_3.4_spmd, body=%wide.region_2.3_spmd.sunk | while | flops 87352896 | bytes 3410213 | solution.py:133
  166.2 0.8 dynamic-slice_bitcast_fusion.2
  168.3 0.8 fusion.83
  169.7 5.9 %fusion.84 = f32[12,8,32,128]{3,2,1,0:T(8,128)} fusion(f32[12,8,32,128]{3,2,1,0:T(8,128)} %get-tuple-element.149, s32[]{:T(128)S(6)} %copy.97, f32[8,8,128]{2,1,0:T(8,128)S(1)} %bitcast.159, f32[8,128]{1,0:T(8,128)} %get-tuple-element.132, f32[8,8,128]{2,1,0:T(8,128)S(1)} %bitcast.160, f32[8,8,128]{2,1,0:T(8,128)S(1)} %bitcast.161, ...), kind=kOutput, calls=%fused_computation.21.clone.1 | convolution fusion | flops 87293952 | bytes 897092 | tf_op jit(solution)/shard_map/while/body/eval_jaxpr/bmnj,bnrj->brm/dot_general | solution.py:131
  177.1 0.8 dynamic-slice_bitcast_fusion.2
  179.2 0.8 fusion.83
  180.6 5.9 %fusion.84 = f32[12,8,32,128]{3,2,1,0:T(8,128)} fusion(f32[12,8,32,128]{3,2,1,0:T(8,128)} %get-tuple-element.149, s32[]{:T(128)S(6)} %copy.97, f32[8,8,128]{2,1,0:T(8,128)S(1)} %bitcast.159, f32[8,128]{1,0:T(8,128)} %get-tuple-element.132, f32[8,8,128]{2,1,0:T(8,128)S(1)} %bitcast.160, f32[8,8,128]{2,1,0:T(8,128)S(1)} %bitcast.161, ...), kind=kOutput, calls=%fused_computation.21.clone.1 | convolution fusion | flops 87293952 | bytes 897092 | tf_op jit(solution)/shard_map/while/body/eval_jaxpr/bmnj,bnrj->brm/dot_general | solution.py:131
  188.0 0.8 dynamic-slice_bitcast_fusion.2
  190.1 0.8 fusion.83
  191.5 5.9 %fusion.84 = f32[12,8,32,128]{3,2,1,0:T(8,128)} fusion(f32[12,8,32,128]{3,2,1,0:T(8,128)} %get-tuple-element.149, s32[]{:T(128)S(6)} %copy.97, f32[8,8,128]{2,1,0:T(8,128)S(1)} %bitcast.159, f32[8,128]{1,0:T(8,128)} %get-tuple-element.132, f32[8,8,128]{2,1,0:T(8,128)S(1)} %bitcast.160, f32[8,8,128]{2,1,0:T(8,128)S(1)} %bitcast.161, ...), kind=kOutput, calls=%fused_computation.21.clone.1 | convolution fusion | flops 87293952 | bytes 897092 | tf_op jit(solution)/shard_map/while/body/eval_jaxpr/bmnj,bnrj->brm/dot_general | solution.py:131
  198.9 0.8 dynamic-slice_bitcast_fusion.2
  201.0 0.8 fusion.83
  202.4 5.9 %fusion.84 = f32[12,8,32,128]{3,2,1,0:T(8,128)} fusion(f32[12,8,32,128]{3,2,1,0:T(8,128)} %get-tuple-element.149, s32[]{:T(128)S(6)} %copy.97, f32[8,8,128]{2,1,0:T(8,128)S(1)} %bitcast.159, f32[8,128]{1,0:T(8,128)} %get-tuple-element.132, f32[8,8,128]{2,1,0:T(8,128)S(1)} %bitcast.160, f32[8,8,128]{2,1,0:T(8,128)S(1)} %bitcast.161, ...), kind=kOutput, calls=%fused_computation.21.clone.1 | convolution fusion | flops 87293952 | bytes 897092 | tf_op jit(solution)/shard_map/while/body/eval_jaxpr/bmnj,bnrj->brm/dot_general | solution.py:131
  209.8 0.8 dynamic-slice_bitcast_fusion.2
  211.9 0.8 fusion.83
  213.3 5.9 %fusion.84 = f32[12,8,32,128]{3,2,1,0:T(8,128)} fusion(f32[12,8,32,128]{3,2,1,0:T(8,128)} %get-tuple-element.149, s32[]{:T(128)S(6)} %copy.97, f32[8,8,128]{2,1,0:T(8,128)S(1)} %bitcast.159, f32[8,128]{1,0:T(8,128)} %get-tuple-element.132, f32[8,8,128]{2,1,0:T(8,128)S(1)} %bitcast.160, f32[8,8,128]{2,1,0:T(8,128)S(1)} %bitcast.161, ...), kind=kOutput, calls=%fused_computation.21.clone.1 | convolution fusion | flops 87293952 | bytes 897092 | tf_op jit(solution)/shard_map/while/body/eval_jaxpr/bmnj,bnrj->brm/dot_general | solution.py:131
  220.6 0.8 dynamic-slice_bitcast_fusion.2
  222.8 0.8 fusion.83
  224.2 5.9 %fusion.84 = f32[12,8,32,128]{3,2,1,0:T(8,128)} fusion(f32[12,8,32,128]{3,2,1,0:T(8,128)} %get-tuple-element.149, s32[]{:T(128)S(6)} %copy.97, f32[8,8,128]{2,1,0:T(8,128)S(1)} %bitcast.159, f32[8,128]{1,0:T(8,128)} %get-tuple-element.132, f32[8,8,128]{2,1,0:T(8,128)S(1)} %bitcast.160, f32[8,8,128]{2,1,0:T(8,128)S(1)} %bitcast.161, ...), kind=kOutput, calls=%fused_computation.21.clone.1 | convolution fusion | flops 87293952 | bytes 897092 | tf_op jit(solution)/shard_map/while/body/eval_jaxpr/bmnj,bnrj->brm/dot_general | solution.py:131
  231.5 0.8 dynamic-slice_bitcast_fusion.2
  233.7 0.8 fusion.83
  235.1 5.9 %fusion.84 = f32[12,8,32,128]{3,2,1,0:T(8,128)} fusion(f32[12,8,32,128]{3,2,1,0:T(8,128)} %get-tuple-element.149, s32[]{:T(128)S(6)} %copy.97, f32[8,8,128]{2,1,0:T(8,128)S(1)} %bitcast.159, f32[8,128]{1,0:T(8,128)} %get-tuple-element.132, f32[8,8,128]{2,1,0:T(8,128)S(1)} %bitcast.160, f32[8,8,128]{2,1,0:T(8,128)S(1)} %bitcast.161, ...), kind=kOutput, calls=%fused_computation.21.clone.1 | convolution fusion | flops 87293952 | bytes 897092 | tf_op jit(solution)/shard_map/while/body/eval_jaxpr/bmnj,bnrj->brm/dot_general | solution.py:131
  242.4 0.8 dynamic-slice_bitcast_fusion.2
  244.6 0.8 fusion.83
  246.0 5.9 %fusion.84 = f32[12,8,32,128]{3,2,1,0:T(8,128)} fusion(f32[12,8,32,128]{3,2,1,0:T(8,128)} %get-tuple-element.149, s32[]{:T(128)S(6)} %copy.97, f32[8,8,128]{2,1,0:T(8,128)S(1)} %bitcast.159, f32[8,128]{1,0:T(8,128)} %get-tuple-element.132, f32[8,8,128]{2,1,0:T(8,128)S(1)} %bitcast.160, f32[8,8,128]{2,1,0:T(8,128)S(1)} %bitcast.161, ...), kind=kOutput, calls=%fused_computation.21.clone.1 | convolution fusion | flops 87293952 | bytes 897092 | tf_op jit(solution)/shard_map/while/body/eval_jaxpr/bmnj,bnrj->brm/dot_general | solution.py:131
  255.4 0.8 fusion.83
  256.9 5.9 %fusion.84 = f32[12,8,32,128]{3,2,1,0:T(8,128)} fusion(f32[12,8,32,128]{3,2,1,0:T(8,128)} %get-tuple-element.149, s32[]{:T(128)S(6)} %copy.97, f32[8,8,128]{2,1,0:T(8,128)S(1)} %bitcast.159, f32[8,128]{1,0:T(8,128)} %get-tuple-element.132, f32[8,8,128]{2,1,0:T(8,128)S(1)} %bitcast.160, f32[8,8,128]{2,1,0:T(8,128)S(1)} %bitcast.161, ...), kind=kOutput, calls=%fused_computation.21.clone.1 | convolution fusion | flops 87293952 | bytes 897092 | tf_op jit(solution)/shard_map/while/body/eval_jaxpr/bmnj,bnrj->brm/dot_general | solution.py:131
  264.2 0.8 dynamic-slice_bitcast_fusion.2
  266.3 0.8 fusion.83
  267.8 5.9 %fusion.84 = f32[12,8,32,128]{3,2,1,0:T(8,128)} fusion(f32[12,8,32,128]{3,2,1,0:T(8,128)} %get-tuple-element.149, s32[]{:T(128)S(6)} %copy.97, f32[8,8,128]{2,1,0:T(8,128)S(1)} %bitcast.159, f32[8,128]{1,0:T(8,128)} %get-tuple-element.132, f32[8,8,128]{2,1,0:T(8,128)S(1)} %bitcast.160, f32[8,8,128]{2,1,0:T(8,128)S(1)} %bitcast.161, ...), kind=kOutput, calls=%fused_computation.21.clone.1 | convolution fusion | flops 87293952 | bytes 897092 | tf_op jit(solution)/shard_map/while/body/eval_jaxpr/bmnj,bnrj->brm/dot_general | solution.py:131
  275.1 0.8 dynamic-slice_bitcast_fusion.2
  277.2 0.8 fusion.83
  278.7 5.9 %fusion.84 = f32[12,8,32,128]{3,2,1,0:T(8,128)} fusion(f32[12,8,32,128]{3,2,1,0:T(8,128)} %get-tuple-element.149, s32[]{:T(128)S(6)} %copy.97, f32[8,8,128]{2,1,0:T(8,128)S(1)} %bitcast.159, f32[8,128]{1,0:T(8,128)} %get-tuple-element.132, f32[8,8,128]{2,1,0:T(8,128)S(1)} %bitcast.160, f32[8,8,128]{2,1,0:T(8,128)S(1)} %bitcast.161, ...), kind=kOutput, calls=%fused_computation.21.clone.1 | convolution fusion | flops 87293952 | bytes 897092 | tf_op jit(solution)/shard_map/while/body/eval_jaxpr/bmnj,bnrj->brm/dot_general | solution.py:131
  288.1 0.8 fusion.83
  289.6 5.9 %fusion.84 = f32[12,8,32,128]{3,2,1,0:T(8,128)} fusion(f32[12,8,32,128]{3,2,1,0:T(8,128)} %get-tuple-element.149, s32[]{:T(128)S(6)} %copy.97, f32[8,8,128]{2,1,0:T(8,128)S(1)} %bitcast.159, f32[8,128]{1,0:T(8,128)} %get-tuple-element.132, f32[8,8,128]{2,1,0:T(8,128)S(1)} %bitcast.160, f32[8,8,128]{2,1,0:T(8,128)S(1)} %bitcast.161, ...), kind=kOutput, calls=%fused_computation.21.clone.1 | convolution fusion | flops 87293952 | bytes 897092 | tf_op jit(solution)/shard_map/while/body/eval_jaxpr/bmnj,bnrj->brm/dot_general | solution.py:131
  295.4 1.1 convolution_bitcast_fusion.3
  296.5 4.3 %fusion.37 = f32[32,96,64]{2,0,1:T(8,128)} fusion(bf16[96,64,64]{2,1,0:T(8,128)(2,1)} %copy.78, f32[32,64]{1,0:T(8,128)S(1)} %convolution_bitcast_fusion.3, bf16[32,64]{1,0:T(8,128)(2,1)} %fusion.33, bf16[1,64,64]{2,1,0:T(8,128)(2,1)} %param.32), kind=kOutput, calls=%fused_computation.60 | convolution fusion | flops 25432064 | bytes 1593344 | tf_op jit(solution)/shard_map/lik,kr->lir/dot_general | solution.py:119
  300.8 1.3 pad_maximum_fusion
  302.1 4.0 %gather_fusion.2 = bf16[576,2048]{1,0:T(8,128)(2,1)} fusion(bf16[288,2048]{1,0:T(8,128)(2,1)S(1)} %pad_maximum_fusion, s32[1024]{0:T(1024)S(1)} %pad_clamp_fusion.3), kind=kCustom, calls=%fused_computation.2 | custom fusion | bytes 4720896 | tf_op jit(solution)/shard_map/jit(_take)/gather | solution.py:110
  306.1 11.7 %gather.23 = bf16[96,6,64,32]{3,2,1,0:T(8,128)(2,1)} reshape(bf16[576,2048]{1,0:T(8,128)(2,1)} %gather_fusion.2) | data formatting | bytes 4718592 | tf_op jit(solution)/shard_map/jit(_take)/gather | solution.py:110
  317.8 10.3 %bitcast_add_fusion.1 = f32[96,32,128]{2,1,0:T(8,128)} fusion(f32[12,8,32,128]{3,2,1,0:T(8,128)} %get-tuple-element.37, bf16[96,64,128]{2,1,0:T(8,128)(2,1)S(1)} %copy-done, f32[32,96,64]{2,0,1:T(8,128)S(1)} %copy-done.1, bf16[96,6,64,64]{3,2,1,0:T(8,128)(2,1)} %copy.71, bf16[96,6,64,32]{3,2,1,0:T(8,128)(2,1)} %gather.23, pred[96,6]{1,0:T(8,128)(4,1)S(1)} %copy-done.6, ...), kind=kOutput, calls=%fused_computation.44 | convolution fusion | flops 204472320 | bytes 12584640 | tf_op jit(solution)/shard_map/lkr,lkm->lrm/dot_general | solution.py:121
  (161 shorter events, 49.6 us)
Async XLA Ops:
  0.0 317.8 %copy-start = (bf16[96,64,128]{2,1,0:T(8,128)(2,1)S(1)}, bf16[96,64,128]{2,1,0:T(8,128)(2,1)}, u32[]{:S(2)}) copy-start(bf16[96,64,128]{2,1,0:T(8,128)(2,1)} %param.25) | copy-start | bytes 4718596
  4.9 295.9 %collective-permute-start.1 = (bf16[96,2048]{1,0:T(8,128)(2,1)}, bf16[96,2048]{1,0:T(8,128)(2,1)}, u32[]{:S(2)}, u32[]{:S(2)}) collective-permute-start(bf16[96,2048]{1,0:T(8,128)(2,1)} %copy.66), channel_id=1, source_target_pairs={{1,0},{2,1},{3,2},{4,3},{5,4},{6,5},{7,6},{8,7},{9,8},{10,9},{11,1... | collective-permute-start | bytes 1179656 | tf_op jit(solution)/shard_map/ppermute | solution.py:23
  14.2 286.6 %collective-permute-start = (bf16[96,2048]{1,0:T(8,128)(2,1)}, bf16[96,2048]{1,0:T(8,128)(2,1)}, u32[]{:S(2)}, u32[]{:S(2)}) collective-permute-start(bf16[96,2048]{1,0:T(8,128)(2,1)} %copy.66), channel_id=1, source_target_pairs={{0,1},{1,2},{2,3},{3,4},{4,5},{5,6},{6,7},{7,8},{8,9},{9,10},{10,1... | collective-permute-start | bytes 1179656 | tf_op jit(solution)/shard_map/ppermute | solution.py:21
  17.4 132.2 %collective-permute-start.6 = (f32[4,7,128]{2,1,0:T(8,128)S(1)}, f32[4,7,128]{2,1,0:T(8,128)S(1)}, u32[]{:S(2)}, u32[]{:S(2)}) collective-permute-start(f32[4,7,128]{2,1,0:T(8,128)S(1)} %get-tuple-element.82), channel_id=1, source_target_pairs={{0,1},{1,2},{2,3},{3,4},{4,5},{5,6},{6,7},{7,8},{8,9},{9,10},{10,1... | collective-permute-start | bytes 43016 | tf_op jit(solution)/shard_map/ppermute | solution.py:21
  19.3 29.0 %copy-start.10 = (s32[1,6]{1,0:T(1,128)S(1)}, s32[1,6]{1,0:T(1,128)}, u32[]{:S(2)}) copy-start(s32[1,6]{1,0:T(1,128)} %param.34) | copy-start | bytes 76
  19.3 29.0 %copy-start.11 = (s32[1,6]{1,0:T(1,128)S(1)}, s32[1,6]{1,0:T(1,128)}, u32[]{:S(2)}) copy-start(s32[1,6]{1,0:T(1,128)} %param.38) | copy-start | bytes 76
  19.3 29.8 %copy-start.9 = (s32[96]{0:T(128)S(1)}, s32[96]{0:T(128)}, u32[]{:S(2)}) copy-start(s32[96]{0:T(128)} %param.30) | copy-start | bytes 1156
  19.3 30.5 %copy-start.7 = (s32[96,6]{0,1:T(8,128)S(1)}, s32[96,6]{0,1:T(8,128)}, u32[]{:S(2)}) copy-start(s32[96,6]{0,1:T(8,128)} %param.29) | copy-start | bytes 6916
  19.3 30.8 %copy-start.4 = (bf16[1,64,64]{2,1,0:T(8,128)(2,1)S(1)}, bf16[1,64,64]{2,1,0:T(8,128)(2,1)}, u32[]{:S(2)}) copy-start(bf16[1,64,64]{2,1,0:T(8,128)(2,1)} %param.31) | copy-start | bytes 24580
  19.3 132.6 %collective-permute-start.7 = (f32[4,7,128]{2,1,0:T(8,128)S(1)}, f32[4,7,128]{2,1,0:T(8,128)S(1)}, u32[]{:S(2)}, u32[]{:S(2)}) collective-permute-start(f32[4,7,128]{2,1,0:T(8,128)S(1)} %get-tuple-element.83), channel_id=1, source_target_pairs={{1,0},{2,1},{3,2},{4,3},{5,4},{6,5},{7,6},{8,7},{9,8},{10,9},{11,1... | collective-permute-start | bytes 43016 | tf_op jit(solution)/shard_map/ppermute | solution.py:23
  31.4 92.7 %copy-start.2 = (bf16[32,64,64]{2,1,0:T(8,128)(2,1)S(1)}, bf16[32,64,64]{2,1,0:T(8,128)(2,1)}, u32[]{:S(2)}) copy-start(bf16[32,64,64]{2,1,0:T(8,128)(2,1)} %param.35) | copy-start | bytes 786436
  31.4 93.7 %copy-start.8 = (s32[96,8]{0,1:T(8,128)S(1)}, s32[96,8]{0,1:T(8,128)}, u32[]{:S(2)}) copy-start(s32[96,8]{0,1:T(8,128)} %param.23) | copy-start | bytes 9220
  33.3 92.9 %copy-start.5 = (bf16[1,64,64]{2,1,0:T(8,128)(2,1)S(1)}, bf16[1,64,64]{2,1,0:T(8,128)(2,1)}, u32[]{:S(2)}) copy-start(bf16[1,64,64]{2,1,0:T(8,128)(2,1)} %param.36) | copy-start | bytes 24580
  46.3 107.6 %collective-permute-start.3 = (bf16[8,2048]{1,0:T(8,128)(2,1)S(1)}, bf16[8,2048]{1,0:T(8,128)(2,1)S(1)}, u32[]{:S(2)}, u32[]{:S(2)}) collective-permute-start(bf16[8,2048]{1,0:T(8,128)(2,1)S(1)} %bitcast.165), channel_id=1, source_target_pairs={{8,0},{16,8},{24,16},{32,24},{40,32},{48,40},{56,48},{64,56},{72,6... | collective-permute-start | bytes 98312 | tf_op jit(solution)/shard_map/ppermute | solution.py:23
  149.5 12.5 %collective-permute-start.2 = (bf16[8,2048]{1,0:T(8,128)(2,1)S(1)}, bf16[8,2048]{1,0:T(8,128)(2,1)S(1)}, u32[]{:S(2)}, u32[]{:S(2)}) collective-permute-start(bf16[8,2048]{1,0:T(8,128)(2,1)S(1)} %bitcast.166), channel_id=1, source_target_pairs={{0,8},{8,16},{16,24},{24,32},{32,40},{40,48},{48,56},{56,64},{64,7... | collective-permute-start | bytes 98312 | tf_op jit(solution)/shard_map/ppermute | solution.py:21
  152.0 11.5 %collective-permute-start.4 = (bf16[4,32,128]{2,1,0:T(8,128)(2,1)S(1)}, bf16[4,32,128]{2,1,0:T(8,128)(2,1)S(1)}, u32[]{:S(2)}, u32[]{:S(2)}) collective-permute-start(bf16[4,32,128]{2,1,0:T(8,128)(2,1)S(1)} %get-tuple-element.80), channel_id=1, source_target_pairs={{0,1},{1,2},{2,3},{3,4},{4,5},{5,6},{6,7},{7,8},{8,9},{9,10},{10,1... | collective-permute-start | bytes 98312 | tf_op jit(solution)/shard_map/ppermute | solution.py:21
  154.0 9.5 %collective-permute-start.5 = (bf16[4,32,128]{2,1,0:T(8,128)(2,1)S(1)}, bf16[4,32,128]{2,1,0:T(8,128)(2,1)S(1)}, u32[]{:S(2)}, u32[]{:S(2)}) collective-permute-start(bf16[4,32,128]{2,1,0:T(8,128)(2,1)S(1)} %get-tuple-element.81), channel_id=1, source_target_pairs={{1,0},{2,1},{3,2},{4,3},{5,4},{6,5},{7,6},{8,7},{9,8},{10,9},{11,1... | collective-permute-start | bytes 98312 | tf_op jit(solution)/shard_map/ppermute | solution.py:23
  306.1 11.7 %copy-start.1 = (f32[32,96,64]{2,0,1:T(8,128)S(1)}, f32[32,96,64]{2,0,1:T(8,128)}, u32[]{:S(2)}) copy-start(f32[32,96,64]{2,0,1:T(8,128)} %fusion.37) | copy-start | bytes 2359300
  306.1 11.7 %copy-start.3 = (bf16[96,6]{1,0:T(8,128)(2,1)S(1)}, bf16[96,6]{1,0:T(8,128)(2,1)}, u32[]{:S(2)}) copy-start(bf16[96,6]{1,0:T(8,128)(2,1)} %fusion.49) | copy-start | bytes 3460
  306.1 11.7 %copy-start.6 = (pred[96,6]{1,0:T(8,128)(4,1)S(1)}, pred[96,6]{1,0:T(8,128)(4,1)}, u32[]{:S(2)}) copy-start(pred[96,6]{1,0:T(8,128)(4,1)} %copy.64) | copy-start | bytes 1732
where the time goes:
time: 331 us; the launch traced here: 328 us
  matrix products  94.2 us (28%)
  local copies, waits for them, and re-layouts  90.2 us (27%)
  blocking collectives  85.2 us (26%)
  starting transfers between devices  35.4 us (11%)
  other arithmetic  22.2 us (7%)
    dot_general x12, matrix products, near_block(): jnp.einsum('bmnj,bnrj->brm', kernel, values, preferred_element_type=wide)  70.5 us
    all_gather x1, blocking collectives, on_device(): lax.all_gather(group_sum.astype(narrow), 'gx', axis=0, tiled=True)  48 us
    ppermute x4, starting transfers between devices, padded(): lax.ppermute(head, axis, [((i + 1) % count, i) for i in range(ends)])  27.2 us
    unnamed x30, local copies, waits for them, and re-layouts  25.5 us
    psum x1, blocking collectives, on_device(): group_sum = lax.psum(mid_term, 'gy')  24.5 us
    gather x2, local copies, waits for them, and re-layouts, on_device(): jnp.take(coeff_rim, leaf_far - (first_leaf - leaves), axis=0)  15.6 us
    all_gather x1, blocking collectives, on_device(): siblings = lax.all_gather(mid_flat, 'gy', axis=0, tiled=True)  12.8 us
    dot_general x1, matrix products, on_device(): jnp.einsum('lkr,lkm->lrm', leaf_field, basis_out, preferred_element_type=...  10.3 us
  transfers between devices with their start and end apart: 8, of which 0 were waited for; matrix products, arithmetic and copies ran while one was open for 53% of the time, Pallas kernels for 0%

commit v1 on v0

--- a/solution.py
+++ b/solution.py
@@ -8,6 +8,18 @@
 BRANCH = 4
 four_pi = 4.0 * math.pi
 leaf_block = 8
+
+
+def group_wires(array_in, shard_axis):
+    chips = jax.lax.axis_size(shard_axis)
+    so_far_all = [chips if rr == 0 else 1 for rr in range(array_in.ndim)]
+    return jax.lax.all_to_all(
+        jnp.tile(array_in, so_far_all),
+        axis_name=shard_axis,
+        split_axis=0,
+        concat_axis=0,
+        tiled=True,
+    )
 
 
 def padded(cells, sides, width):
@@ -86,7 +98,7 @@
     group_sum = lax.psum(mid_term, "gy")
     nearby = padded(siblings, (("gx", 0),), group_size)
     mid_picked = jnp.take(nearby, cluster_far[0] - (gx_index - 1) * group_size, axis=0)
-    top_coeffs = lax.all_gather(group_sum.astype(narrow), "gx", axis=0, tiled=True)
+    top_coeffs = group_wires(group_sum.astype(narrow), "gx")
     top_block = top_coeffs.reshape(groups, coeff_order, columns)
     root_terms = jnp.einsum("gik,gkr->gir", group_up, top_block, preferred_element_type=wide)
     root_coeffs = jnp.sum(

time: 331 us -> 296 us (0.89)
  blocking collectives: 85.2 us -> 36.7 us
  other arithmetic: 22.2 us -> 27.5 us
  local copies, waits for them, and re-layouts: 90.2 us -> 95 us
    all_gather x1 -> x0, blocking collectives: 48 us -> none  [on_device(): lax.all_gather(group_sum.astype(narrow), 'gx', axis=0, tiled=True)]
    all_to_all x0 -> x1, starting transfers between devices: none -> 5.65 us  [group_wires(): jax.lax.all_to_all(jnp.tile(array_in, so_far_all), axis_name=shard_axis,...]
    unnamed x30 -> x36, local copies, waits for them, and re-layouts: 25.5 us -> 28.2 us
  transfers between devices with their start and end apart: 8 -> 9, of which waited for: 0 -> 0; matrix products, arithmetic and copies ran while one was open for 53% -> 63% of each run, Pallas kernels for 0% -> 0%
where the time goes in v1:
time: 296 us; the launch traced here: 292 us
  local copies, waits for them, and re-layouts  95 us (32%)
  matrix products  94 us (32%)
  starting transfers between devices  38.5 us (13%)
  blocking collectives  36.7 us (12%)
  other arithmetic  27.5 us (9%)
    dot_general x12, matrix products, near_block(): jnp.einsum('bmnj,bnrj->brm', kernel, values, preferred_element_type=wide)  70.5 us
    unnamed x36, local copies, waits for them, and re-layouts  28.2 us
    ppermute x4, starting transfers between devices, padded(): lax.ppermute(head, axis, [((i + 1) % count, i) for i in range(ends)])  24.5 us
    psum x1, blocking collectives, on_device(): group_sum = lax.psum(mid_term, 'gy')  23.9 us
    gather x2, local copies, waits for them, and re-layouts, on_device(): jnp.take(coeff_rim, leaf_far - (first_leaf - leaves), axis=0)  15.6 us
    all_gather x1, blocking collectives, on_device(): siblings = lax.all_gather(mid_flat, 'gy', axis=0, tiled=True)  12.8 us
    dot_general x1, matrix products, on_device(): jnp.einsum('lkr,lkm->lrm', leaf_field, basis_out, preferred_element_type=...  10.3 us
    slice x12, local copies, waits for them, and re-layouts, near_kernel(): panel_area = source[:, None, :, 6, :]  9.31 us
  transfers between devices with their start and end apart: 9, of which 0 were waited for; matrix products, arithmetic and copies ran while one was open for 63% of the time, Pallas kernels for 0%

profile of v1, /device:TPU:8, one launch (start us, length us, event | category | flops | bytes accessed | tf_op | source)
XLA Modules:
  0.0 292.4 jit_solution(941053071900236881)
XLA Ops:
  0.0 2.6 convolution_convert_fusion
  2.6 1.3 copy.65
  4.0 0.9 copy.66
  4.9 9.3 %collective-permute-start.1 = (bf16[96,2048]{1,0:T(8,128)(2,1)}, bf16[96,2048]{1,0:T(8,128)(2,1)}, u32[]{:S(2)}, u32[]{:S(2)}) collective-permute-start(bf16[96,2048]{1,0:T(8,128)(2,1)} %copy.66), channel_id=1, source_target_pairs={{1,0},{2,1},{3,2},{4,3},{5,4},{6,5},{7,6},{8,7},{9,8},{10,9},{11,1... | collective-permute-start | bytes 1179656 | tf_op jit(solution)/shard_map/ppermute | solution.py:35
  14.2 1.9 collective-permute-start
  16.1 0.8 fusion.62
  16.9 1.9 collective-permute-start.4
  18.8 1.2 copy.80
  20.0 1.9 collective-permute-start.6
  22.0 7.9 %collective-permute-start.7 = (f32[4,7,128]{2,1,0:T(8,128)S(1)}, f32[4,7,128]{2,1,0:T(8,128)S(1)}, u32[]{:S(2)}, u32[]{:S(2)}) collective-permute-start(f32[4,7,128]{2,1,0:T(8,128)S(1)} %get-tuple-element.83), channel_id=1, source_target_pairs={{1,0},{2,1},{3,2},{4,3},{5,4},{6,5},{7,6},{8,7},{9,8},{10,9},{11,1... | collective-permute-start | bytes 43016 | tf_op jit(solution)/shard_map/ppermute | solution.py:35
  29.8 4.0 %copy.72 = bf16[96,64,64]{2,1,0:T(8,128)(2,1)} copy(bf16[96,64,64]{0,2,1:T(8,128)(2,1)} %param.26) | data formatting | bytes 1572864 | tf_op args[5]
  33.9 2.0 fusion.35
  36.2 23.9 %psum.7 = bf16[1,2048]{1,0:T(2,128)(2,1)S(1)} all-reduce(f32[1,2048]{1,0:T(1,128)S(1)} %reshape.199), channel_id=1, replica_groups=mesh['gx'=32,'gy'=8] {'gy'}, use_global_device_ids=true, to_apply=%region_0.0 | all-reduce | flops 2048 | bytes 12288 | tf_op jit(solution)/shard_map/psum | solution.py:98
  60.8 1.4 reduce.3
  62.9 5.6 %all-to-all-start = ((bf16[32,2,1024]{2,1,0:T(2,128)(2,1)}), bf16[32,2,1024]{2,1,0:T(2,128)(2,1)}, u32[]{:S(2)}, u32[]{:S(2)}) async-start(bf16[32,2,1024]{2,1,0:T(2,128)(2,1)} %reshape.262), calls=%async_computation | async-start | bytes 262144 | tf_op jit(solution)/shard_map/all_to_all | solution.py:16
  73.6 12.8 %all-gather = bf16[8,1,2048]{2,1,0:T(2,128)(2,1)S(1)} all-gather(bf16[1,1,2048]{2,1,0:T(2,128)(2,1)S(1)} %reshape.250), channel_id=1, replica_groups=mesh['gx'=32,'gy'=8] {'gy'}, dimensions={0}, use_global_device_ids=true | all-gather | bytes 36864 | tf_op jit(solution)/shard_map/all_gather | solution.py:97
  86.9 4.0 %copy.78 = bf16[96,64,64]{2,1,0:T(8,128)(2,1)} copy(bf16[96,64,64]{0,2,1:T(8,128)(2,1)} %param.27) | data formatting | bytes 1572864 | tf_op args[6]
  90.9 16.1 %copy.71 = bf16[96,6,64,64]{3,2,1,0:T(8,128)(2,1)} copy(bf16[96,6,64,64]{0,3,2,1:T(8,128)(2,1)} %param.28) | data formatting | bytes 9437184 | tf_op args[7]
  107.0 4.0 %collective-permute-start.5 = (bf16[4,32,128]{2,1,0:T(8,128)(2,1)S(1)}, bf16[4,32,128]{2,1,0:T(8,128)(2,1)S(1)}, u32[]{:S(2)}, u32[]{:S(2)}) collective-permute-start(bf16[4,32,128]{2,1,0:T(8,128)(2,1)S(1)} %get-tuple-element.81), channel_id=1, source_target_pairs={{1,0},{2,1},{3,2},{4,3},{5,4},{6,5},{7,6},{8,7},{9,8},{10,9},{11,1... | collective-permute-start | bytes 98312 | tf_op jit(solution)/shard_map/ppermute | solution.py:35
  111.0 3.4 %collective-permute-start.3 = (bf16[8,2048]{1,0:T(8,128)(2,1)}, bf16[8,2048]{1,0:T(8,128)(2,1)}, u32[]{:S(2)}, u32[]{:S(2)}) collective-permute-start(bf16[8,2048]{1,0:T(8,128)(2,1)} %bitcast.123), channel_id=1, source_target_pairs={{8,0},{16,8},{24,16},{32,24},{40,32},{48,40},{56,48},{64,56},{72,6... | collective-permute-start | bytes 98312 | tf_op jit(solution)/shard_map/ppermute | solution.py:35
  114.4 2.7 collective-permute-start.2
  117.1 1.2 pad_maximum_fusion.1
  118.4 130.7 %while.10 = (s32[]{:T(128)}, f32[12,8,32,128]{3,2,1,0:T(8,128)}, s32[12,8,8]{2,1,0:T(8,128)}, bf16[104,32,128]{2,1,0:T(8,128)(2,1)S(1)}, f32[104,7,128]{2,1,0:T(...) while((s32[]{:T(128)}, f32[12,8,32,128]{3,2,1,0:T(8,128)}, s32[12,8,8]{2,1,0:T(8,128)}, ...), condition=%wide.region_3.4_spmd, body=%wide.region_2.3_spmd.sunk | while | flops 87352896 | bytes 3410213 | solution.py:145
  119.8 0.8 dynamic-slice_bitcast_fusion.2
  121.9 0.8 fusion.83
  123.4 5.9 %fusion.84 = f32[12,8,32,128]{3,2,1,0:T(8,128)} fusion(f32[12,8,32,128]{3,2,1,0:T(8,128)} %get-tuple-element.149, s32[]{:T(128)S(6)} %copy.97, f32[8,8,128]{2,1,0:T(8,128)S(1)} %bitcast.156, f32[8,128]{1,0:T(8,128)} %get-tuple-element.132, f32[8,8,128]{2,1,0:T(8,128)S(1)} %bitcast.157, f32[8,8,128]{2,1,0:T(8,128)S(1)} %bitcast.158, ...), kind=kOutput, calls=%fused_computation.21.clone.1 | convolution fusion | flops 87293952 | bytes 897092 | tf_op jit(solution)/shard_map/while/body/eval_jaxpr/bmnj,bnrj->brm/dot_general | solution.py:143
  130.7 0.8 dynamic-slice_bitcast_fusion.2
  132.8 0.8 fusion.83
  134.3 5.9 %fusion.84 = f32[12,8,32,128]{3,2,1,0:T(8,128)} fusion(f32[12,8,32,128]{3,2,1,0:T(8,128)} %get-tuple-element.149, s32[]{:T(128)S(6)} %copy.97, f32[8,8,128]{2,1,0:T(8,128)S(1)} %bitcast.156, f32[8,128]{1,0:T(8,128)} %get-tuple-element.132, f32[8,8,128]{2,1,0:T(8,128)S(1)} %bitcast.157, f32[8,8,128]{2,1,0:T(8,128)S(1)} %bitcast.158, ...), kind=kOutput, calls=%fused_computation.21.clone.1 | convolution fusion | flops 87293952 | bytes 897092 | tf_op jit(solution)/shard_map/while/body/eval_jaxpr/bmnj,bnrj->brm/dot_general | solution.py:143
  143.7 0.8 fusion.83
  145.2 5.9 %fusion.84 = f32[12,8,32,128]{3,2,1,0:T(8,128)} fusion(f32[12,8,32,128]{3,2,1,0:T(8,128)} %get-tuple-element.149, s32[]{:T(128)S(6)} %copy.97, f32[8,8,128]{2,1,0:T(8,128)S(1)} %bitcast.156, f32[8,128]{1,0:T(8,128)} %get-tuple-element.132, f32[8,8,128]{2,1,0:T(8,128)S(1)} %bitcast.157, f32[8,8,128]{2,1,0:T(8,128)S(1)} %bitcast.158, ...), kind=kOutput, calls=%fused_computation.21.clone.1 | convolution fusion | flops 87293952 | bytes 897092 | tf_op jit(solution)/shard_map/while/body/eval_jaxpr/bmnj,bnrj->brm/dot_general | solution.py:143
  154.6 0.8 fusion.83
  156.1 5.9 %fusion.84 = f32[12,8,32,128]{3,2,1,0:T(8,128)} fusion(f32[12,8,32,128]{3,2,1,0:T(8,128)} %get-tuple-element.149, s32[]{:T(128)S(6)} %copy.97, f32[8,8,128]{2,1,0:T(8,128)S(1)} %bitcast.156, f32[8,128]{1,0:T(8,128)} %get-tuple-element.132, f32[8,8,128]{2,1,0:T(8,128)S(1)} %bitcast.157, f32[8,8,128]{2,1,0:T(8,128)S(1)} %bitcast.158, ...), kind=kOutput, calls=%fused_computation.21.clone.1 | convolution fusion | flops 87293952 | bytes 897092 | tf_op jit(solution)/shard_map/while/body/eval_jaxpr/bmnj,bnrj->brm/dot_general | solution.py:143
  165.5 0.8 fusion.83
  167.0 5.9 %fusion.84 = f32[12,8,32,128]{3,2,1,0:T(8,128)} fusion(f32[12,8,32,128]{3,2,1,0:T(8,128)} %get-tuple-element.149, s32[]{:T(128)S(6)} %copy.97, f32[8,8,128]{2,1,0:T(8,128)S(1)} %bitcast.156, f32[8,128]{1,0:T(8,128)} %get-tuple-element.132, f32[8,8,128]{2,1,0:T(8,128)S(1)} %bitcast.157, f32[8,8,128]{2,1,0:T(8,128)S(1)} %bitcast.158, ...), kind=kOutput, calls=%fused_computation.21.clone.1 | convolution fusion | flops 87293952 | bytes 897092 | tf_op jit(solution)/shard_map/while/body/eval_jaxpr/bmnj,bnrj->brm/dot_general | solution.py:143
  176.4 0.8 fusion.83
  177.8 5.9 %fusion.84 = f32[12,8,32,128]{3,2,1,0:T(8,128)} fusion(f32[12,8,32,128]{3,2,1,0:T(8,128)} %get-tuple-element.149, s32[]{:T(128)S(6)} %copy.97, f32[8,8,128]{2,1,0:T(8,128)S(1)} %bitcast.156, f32[8,128]{1,0:T(8,128)} %get-tuple-element.132, f32[8,8,128]{2,1,0:T(8,128)S(1)} %bitcast.157, f32[8,8,128]{2,1,0:T(8,128)S(1)} %bitcast.158, ...), kind=kOutput, calls=%fused_computation.21.clone.1 | convolution fusion | flops 87293952 | bytes 897092 | tf_op jit(solution)/shard_map/while/body/eval_jaxpr/bmnj,bnrj->brm/dot_general | solution.py:143
  187.3 0.8 fusion.83
  188.7 5.9 %fusion.84 = f32[12,8,32,128]{3,2,1,0:T(8,128)} fusion(f32[12,8,32,128]{3,2,1,0:T(8,128)} %get-tuple-element.149, s32[]{:T(128)S(6)} %copy.97, f32[8,8,128]{2,1,0:T(8,128)S(1)} %bitcast.156, f32[8,128]{1,0:T(8,128)} %get-tuple-element.132, f32[8,8,128]{2,1,0:T(8,128)S(1)} %bitcast.157, f32[8,8,128]{2,1,0:T(8,128)S(1)} %bitcast.158, ...), kind=kOutput, calls=%fused_computation.21.clone.1 | convolution fusion | flops 87293952 | bytes 897092 | tf_op jit(solution)/shard_map/while/body/eval_jaxpr/bmnj,bnrj->brm/dot_general | solution.py:143
  198.2 0.8 fusion.83
  199.6 5.9 %fusion.84 = f32[12,8,32,128]{3,2,1,0:T(8,128)} fusion(f32[12,8,32,128]{3,2,1,0:T(8,128)} %get-tuple-element.149, s32[]{:T(128)S(6)} %copy.97, f32[8,8,128]{2,1,0:T(8,128)S(1)} %bitcast.156, f32[8,128]{1,0:T(8,128)} %get-tuple-element.132, f32[8,8,128]{2,1,0:T(8,128)S(1)} %bitcast.157, f32[8,8,128]{2,1,0:T(8,128)S(1)} %bitcast.158, ...), kind=kOutput, calls=%fused_computation.21.clone.1 | convolution fusion | flops 87293952 | bytes 897092 | tf_op jit(solution)/shard_map/while/body/eval_jaxpr/bmnj,bnrj->brm/dot_general | solution.py:143
  209.1 0.8 fusion.83
  210.5 5.9 %fusion.84 = f32[12,8,32,128]{3,2,1,0:T(8,128)} fusion(f32[12,8,32,128]{3,2,1,0:T(8,128)} %get-tuple-element.149, s32[]{:T(128)S(6)} %copy.97, f32[8,8,128]{2,1,0:T(8,128)S(1)} %bitcast.156, f32[8,128]{1,0:T(8,128)} %get-tuple-element.132, f32[8,8,128]{2,1,0:T(8,128)S(1)} %bitcast.157, f32[8,8,128]{2,1,0:T(8,128)S(1)} %bitcast.158, ...), kind=kOutput, calls=%fused_computation.21.clone.1 | convolution fusion | flops 87293952 | bytes 897092 | tf_op jit(solution)/shard_map/while/body/eval_jaxpr/bmnj,bnrj->brm/dot_general | solution.py:143
  217.9 0.8 dynamic-slice_bitcast_fusion.2
  220.0 0.8 fusion.83
  221.4 5.9 %fusion.84 = f32[12,8,32,128]{3,2,1,0:T(8,128)} fusion(f32[12,8,32,128]{3,2,1,0:T(8,128)} %get-tuple-element.149, s32[]{:T(128)S(6)} %copy.97, f32[8,8,128]{2,1,0:T(8,128)S(1)} %bitcast.156, f32[8,128]{1,0:T(8,128)} %get-tuple-element.132, f32[8,8,128]{2,1,0:T(8,128)S(1)} %bitcast.157, f32[8,8,128]{2,1,0:T(8,128)S(1)} %bitcast.158, ...), kind=kOutput, calls=%fused_computation.21.clone.1 | convolution fusion | flops 87293952 | bytes 897092 | tf_op jit(solution)/shard_map/while/body/eval_jaxpr/bmnj,bnrj->brm/dot_general | solution.py:143
  230.9 0.8 fusion.83
  232.3 5.9 %fusion.84 = f32[12,8,32,128]{3,2,1,0:T(8,128)} fusion(f32[12,8,32,128]{3,2,1,0:T(8,128)} %get-tuple-element.149, s32[]{:T(128)S(6)} %copy.97, f32[8,8,128]{2,1,0:T(8,128)S(1)} %bitcast.156, f32[8,128]{1,0:T(8,128)} %get-tuple-element.132, f32[8,8,128]{2,1,0:T(8,128)S(1)} %bitcast.157, f32[8,8,128]{2,1,0:T(8,128)S(1)} %bitcast.158, ...), kind=kOutput, calls=%fused_computation.21.clone.1 | convolution fusion | flops 87293952 | bytes 897092 | tf_op jit(solution)/shard_map/while/body/eval_jaxpr/bmnj,bnrj->brm/dot_general | solution.py:143
  241.7 0.8 fusion.83
  243.2 5.9 %fusion.84 = f32[12,8,32,128]{3,2,1,0:T(8,128)} fusion(f32[12,8,32,128]{3,2,1,0:T(8,128)} %get-tuple-element.149, s32[]{:T(128)S(6)} %copy.97, f32[8,8,128]{2,1,0:T(8,128)S(1)} %bitcast.156, f32[8,128]{1,0:T(8,128)} %get-tuple-element.132, f32[8,8,128]{2,1,0:T(8,128)S(1)} %bitcast.157, f32[8,8,128]{2,1,0:T(8,128)S(1)} %bitcast.158, ...), kind=kOutput, calls=%fused_computation.21.clone.1 | convolution fusion | flops 87293952 | bytes 897092 | tf_op jit(solution)/shard_map/while/body/eval_jaxpr/bmnj,bnrj->brm/dot_general | solution.py:143
  249.1 0.9 pad_maximum_fusion.3
  250.7 0.8 broadcast_select_fusion.1
  251.6 1.7 convolution_bitcast_fusion.3
  253.3 1.4 reshape.263
  255.4 1.2 reshape.200
  256.6 1.6 bitcast_reduce_fusion
  258.2 1.7 gather_fusion.4
  260.0 1.1 convolution_bitcast_fusion.1
  261.1 1.2 fusion.33
  262.4 2.8 fusion.37
  265.1 1.3 pad_maximum_fusion
  266.5 4.0 %gather_fusion.2 = bf16[576,2048]{1,0:T(8,128)(2,1)} fusion(bf16[288,2048]{1,0:T(8,128)(2,1)S(1)} %pad_maximum_fusion, s32[1024]{0:T(1024)S(1)} %pad_clamp_fusion.3), kind=kCustom, calls=%fused_computation.2 | custom fusion | bytes 4720896 | tf_op jit(solution)/shard_map/jit(_take)/gather | solution.py:122
  270.4 11.7 %gather.23 = bf16[96,6,64,32]{3,2,1,0:T(8,128)(2,1)} reshape(bf16[576,2048]{1,0:T(8,128)(2,1)} %gather_fusion.2) | data formatting | bytes 4718592 | tf_op jit(solution)/shard_map/jit(_take)/gather | solution.py:122
  282.1 10.3 %bitcast_add_fusion.1 = f32[96,32,128]{2,1,0:T(8,128)} fusion(f32[12,8,32,128]{3,2,1,0:T(8,128)} %get-tuple-element.37, bf16[96,64,128]{2,1,0:T(8,128)(2,1)S(1)} %copy-done, f32[32,96,64]{2,0,1:T(8,128)S(1)} %copy-done.2, bf16[96,6,64,64]{3,2,1,0:T(8,128)(2,1)} %copy.71, bf16[96,6,64,32]{3,2,1,0:T(8,128)(2,1)} %gather.23, pred[96,6]{1,0:T(8,128)(4,1)S(1)} %copy-done.7, ...), kind=kOutput, calls=%fused_computation.44 | convolution fusion | flops 204472320 | bytes 12584640 | tf_op jit(solution)/shard_map/lkr,lkm->lrm/dot_general | solution.py:133
  (172 shorter events, 57.3 us)
Async XLA Ops:
  0.0 282.1 %copy-start = (bf16[96,64,128]{2,1,0:T(8,128)(2,1)S(1)}, bf16[96,64,128]{2,1,0:T(8,128)(2,1)}, u32[]{:S(2)}) copy-start(bf16[96,64,128]{2,1,0:T(8,128)(2,1)} %param.25) | copy-start | bytes 4718596
  4.9 260.2 %collective-permute-start.1 = (bf16[96,2048]{1,0:T(8,128)(2,1)}, bf16[96,2048]{1,0:T(8,128)(2,1)}, u32[]{:S(2)}, u32[]{:S(2)}) collective-permute-start(bf16[96,2048]{1,0:T(8,128)(2,1)} %copy.66), channel_id=1, source_target_pairs={{1,0},{2,1},{3,2},{4,3},{5,4},{6,5},{7,6},{8,7},{9,8},{10,9},{11,1... | collective-permute-start | bytes 1179656 | tf_op jit(solution)/shard_map/ppermute | solution.py:35
  14.2 250.9 %collective-permute-start = (bf16[96,2048]{1,0:T(8,128)(2,1)}, bf16[96,2048]{1,0:T(8,128)(2,1)}, u32[]{:S(2)}, u32[]{:S(2)}) collective-permute-start(bf16[96,2048]{1,0:T(8,128)(2,1)} %copy.66), channel_id=1, source_target_pairs={{0,1},{1,2},{2,3},{3,4},{4,5},{5,6},{6,7},{7,8},{8,9},{9,10},{10,1... | collective-permute-start | bytes 1179656 | tf_op jit(solution)/shard_map/ppermute | solution.py:33
  16.9 97.5 %collective-permute-start.4 = (bf16[4,32,128]{2,1,0:T(8,128)(2,1)S(1)}, bf16[4,32,128]{2,1,0:T(8,128)(2,1)S(1)}, u32[]{:S(2)}, u32[]{:S(2)}) collective-permute-start(bf16[4,32,128]{2,1,0:T(8,128)(2,1)S(1)} %get-tuple-element.80), channel_id=1, source_target_pairs={{0,1},{1,2},{2,3},{3,4},{4,5},{5,6},{6,7},{7,8},{8,9},{9,10},{10,1... | collective-permute-start | bytes 98312 | tf_op jit(solution)/shard_map/ppermute | solution.py:33
  20.0 87.0 %collective-permute-start.6 = (f32[4,7,128]{2,1,0:T(8,128)S(1)}, f32[4,7,128]{2,1,0:T(8,128)S(1)}, u32[]{:S(2)}, u32[]{:S(2)}) collective-permute-start(f32[4,7,128]{2,1,0:T(8,128)S(1)} %get-tuple-element.82), channel_id=1, source_target_pairs={{0,1},{1,2},{2,3},{3,4},{4,5},{5,6},{6,7},{7,8},{8,9},{9,10},{10,1... | collective-permute-start | bytes 43016 | tf_op jit(solution)/shard_map/ppermute | solution.py:33
  22.0 13.9 %copy-start.6 = (bf16[1,64,64]{2,1,0:T(8,128)(2,1)S(1)}, bf16[1,64,64]{2,1,0:T(8,128)(2,1)}, u32[]{:S(2)}) copy-start(bf16[1,64,64]{2,1,0:T(8,128)(2,1)} %param.31) | copy-start | bytes 24580
  22.0 89.0 %collective-permute-start.7 = (f32[4,7,128]{2,1,0:T(8,128)S(1)}, f32[4,7,128]{2,1,0:T(8,128)S(1)}, u32[]{:S(2)}, u32[]{:S(2)}) collective-permute-start(f32[4,7,128]{2,1,0:T(8,128)S(1)} %get-tuple-element.83), channel_id=1, source_target_pairs={{1,0},{2,1},{3,2},{4,3},{5,4},{6,5},{7,6},{8,7},{9,8},{10,9},{11,1... | collective-permute-start | bytes 43016 | tf_op jit(solution)/shard_map/ppermute | solution.py:35
  33.8 34.7 %copy-start.11 = (s32[1,6]{1,0:T(1,128)S(1)}, s32[1,6]{1,0:T(1,128)}, u32[]{:S(2)}) copy-start(s32[1,6]{1,0:T(1,128)} %param.34) | copy-start | bytes 76
  33.9 35.4 %copy-start.12 = (s32[1,6]{1,0:T(1,128)S(1)}, s32[1,6]{1,0:T(1,128)}, u32[]{:S(2)}) copy-start(s32[1,6]{1,0:T(1,128)} %param.38) | copy-start | bytes 76
  33.9 37.1 %copy-start.8 = (s32[96,6]{0,1:T(8,128)S(1)}, s32[96,6]{0,1:T(8,128)}, u32[]{:S(2)}) copy-start(s32[96,6]{0,1:T(8,128)} %param.29) | copy-start | bytes 6916
  33.9 37.9 %copy-start.10 = (s32[96]{0:T(128)S(1)}, s32[96]{0:T(128)}, u32[]{:S(2)}) copy-start(s32[96]{0:T(128)} %param.30) | copy-start | bytes 1156
  33.9 38.5 %copy-start.9 = (s32[96,8]{0,1:T(8,128)S(1)}, s32[96,8]{0,1:T(8,128)}, u32[]{:S(2)}) copy-start(s32[96,8]{0,1:T(8,128)} %param.23) | copy-start | bytes 9220
  62.9 190.4 %all-to-all-start = ((bf16[32,2,1024]{2,1,0:T(2,128)(2,1)}), bf16[32,2,1024]{2,1,0:T(2,128)(2,1)}, u32[]{:S(2)}, u32[]{:S(2)}) async-start(bf16[32,2,1024]{2,1,0:T(2,128)(2,1)} %reshape.262), calls=%async_computation | async-start | bytes 262144 | tf_op jit(solution)/shard_map/all_to_all | solution.py:16
  107.0 10.1 %collective-permute-start.5 = (bf16[4,32,128]{2,1,0:T(8,128)(2,1)S(1)}, bf16[4,32,128]{2,1,0:T(8,128)(2,1)S(1)}, u32[]{:S(2)}, u32[]{:S(2)}) collective-permute-start(bf16[4,32,128]{2,1,0:T(8,128)(2,1)S(1)} %get-tuple-element.81), channel_id=1, source_target_pairs={{1,0},{2,1},{3,2},{4,3},{5,4},{6,5},{7,6},{8,7},{9,8},{10,9},{11,1... | collective-permute-start | bytes 98312 | tf_op jit(solution)/shard_map/ppermute | solution.py:35
  111.0 138.1 %collective-permute-start.3 = (bf16[8,2048]{1,0:T(8,128)(2,1)}, bf16[8,2048]{1,0:T(8,128)(2,1)}, u32[]{:S(2)}, u32[]{:S(2)}) collective-permute-start(bf16[8,2048]{1,0:T(8,128)(2,1)} %bitcast.123), channel_id=1, source_target_pairs={{8,0},{16,8},{24,16},{32,24},{40,32},{48,40},{56,48},{64,56},{72,6... | collective-permute-start | bytes 98312 | tf_op jit(solution)/shard_map/ppermute | solution.py:35
  114.4 134.6 %collective-permute-start.2 = (bf16[8,2048]{1,0:T(8,128)(2,1)}, bf16[8,2048]{1,0:T(8,128)(2,1)}, u32[]{:S(2)}, u32[]{:S(2)}) collective-permute-start(bf16[8,2048]{1,0:T(8,128)(2,1)} %bitcast.123), channel_id=1, source_target_pairs={{0,8},{8,16},{16,24},{24,32},{32,40},{40,48},{48,56},{56,64},{64,7... | collective-permute-start | bytes 98312 | tf_op jit(solution)/shard_map/ppermute | solution.py:33
  249.1 10.9 %copy-start.13 = (pred[6]{0:T(512)(128)(4,1)S(1)}, pred[6]{0:T(512)(128)(4,1)}, u32[]{:S(2)}) copy-start(pred[6]{0:T(512)(128)(4,1)} %compare_and_fusion.2) | copy-start | bytes 22
  249.1 13.3 %copy-start.1 = (bf16[96,64,64]{2,1,0:T(8,128)(2,1)S(1)}, bf16[96,64,64]{2,1,0:T(8,128)(2,1)}, u32[]{:S(2)}) copy-start(bf16[96,64,64]{2,1,0:T(8,128)(2,1)} %copy.78) | copy-start | bytes 2359300
  255.4 7.0 %copy-start.3 = (f32[32,64]{1,0:T(8,128)S(1)}, f32[32,64]{1,0:T(8,128)}, u32[]{:S(2)}) copy-start(f32[32,64]{1,0:T(8,128)} %convolution_bitcast_fusion.3) | copy-start | bytes 24580
  255.4 7.0 %copy-start.5 = (bf16[1,64,64]{2,1,0:T(8,128)(2,1)S(1)}, bf16[1,64,64]{2,1,0:T(8,128)(2,1)}, u32[]{:S(2)}) copy-start(bf16[1,64,64]{2,1,0:T(8,128)(2,1)} %param.32) | copy-start | bytes 24580
  270.4 11.7 %copy-start.2 = (f32[32,96,64]{2,0,1:T(8,128)S(1)}, f32[32,96,64]{2,0,1:T(8,128)}, u32[]{:S(2)}) copy-start(f32[32,96,64]{2,0,1:T(8,128)} %fusion.37) | copy-start | bytes 2359300
  270.4 11.7 %copy-start.4 = (bf16[96,6]{1,0:T(8,128)(2,1)S(1)}, bf16[96,6]{1,0:T(8,128)(2,1)}, u32[]{:S(2)}) copy-start(bf16[96,6]{1,0:T(8,128)(2,1)} %fusion.49) | copy-start | bytes 3460
  270.4 11.7 %copy-start.7 = (pred[96,6]{1,0:T(8,128)(4,1)S(1)}, pred[96,6]{1,0:T(8,128)(4,1)}, u32[]{:S(2)}) copy-start(pred[96,6]{1,0:T(8,128)(4,1)} %copy.64) | copy-start | bytes 1732
